TPU v7x, 32 devices: a whole 2x2x4 slice. The times are simulated.
32 devices in a mesh: sub: 8 (over z, y), blk: 4 (over x, core).
Axes of the slice: x: 2, y: 2, z: 4, core: 2. Of those that a mesh axis runs over, the one named last changes fastest.
Arguments:
- initial_state: float32 [8, 64, 2048], P('sub', None, 'blk'), may hold values from -6 to 6
- source: bfloat16 [8, 8, 64, 2048], P('sub', None, None, 'blk'), may hold values from -6 to 6
- inverse_diag: float32 [8, 2048], P('sub', 'blk'), may hold values from 0.5 to 0.85
- inverse_off: bfloat16 [8, 2048, 2048], P('sub', None, 'blk'), may hold values from -0.032958984 to 0.032958984
- coupling: float32 [8, 128], P('sub', 'blk'), may hold values from 0.3 to 3
- initial_waves: bfloat16 [8, 128, 512], P('sub', 'blk'), may hold values from -6 to 6
- bucket: int32 [8], P('sub'), may hold values from 0 to 2
- partner: int32 [8, 128], P('sub', 'blk'), may hold values from 0 to 7
- position_of: int32 [8], replicated, may hold values from 0 to 7, each once
Outputs:
- last_state: float32 [8, 64, 2048], P('sub', None, 'blk')
- waveform: float32 [8, 128, 512], P('sub', 'blk')
Inputs may be any that keep to these rules, and one draw needn't show every extreme that they name: A subcircuit of bucket b takes 8 / 2 ** (2 - b) implicit Euler steps. `position_of`: a permutation.
All inputs are finite; a program needn't handle non-finite values.
Results may differ from a plain program's by a relative error of at most 0.0052.
Values may be sent and summed in bfloat16 or wider, within the bound.
A program may use at most 64 MiB of HBM per device.

v0:
```python
import jax
import jax.numpy as jnp
from jax import lax
from jax.sharding import PartitionSpec as P

SWEEPS = 2


def step_count(bucket, refined_points):
    return jnp.where(
        bucket == 0,
        refined_points // 4,
        jnp.where(bucket == 1, refined_points // 2, refined_points),
    ).astype(jnp.int32)


def port_fetch(waves, selector):
    return jnp.einsum(
        "qjr,rjc->qjc",
        selector,
        lax.all_gather(waves, "sub", axis=0, tiled=True),
        preferred_element_type=jnp.float32,
    ).astype(jnp.bfloat16)


def spread_ports(injected, stride):
    padded = jnp.pad(injected[..., None], [(0, 0)] * injected.ndim + [(0, stride - 1)])
    return padded.reshape(injected.shape[:-1] + (injected.shape[-1] * stride,))


def run_together(
    initial_state, source, inverse_diag, inverse_off, coupling, step_total, spacing, incoming
):
    sub_dev, corners, node_block = initial_state.shape
    refined_points = source.shape[1]
    ports_block = coupling.shape[1]
    stride = node_block // ports_block
    spacing_float = spacing.astype(jnp.float32)
    driven = incoming.astype(jnp.float32).reshape(sub_dev, ports_block, refined_points, corners)
    points = jnp.arange(refined_points, dtype=jnp.int32)

    def contract(totals, shard_rows):
        return totals + jnp.einsum(
            "qcn,qnm->qcm", shard_rows, inverse_off, preferred_element_type=jnp.float32
        )

    def advance(time_step_index, carried):
        current, sample_times = carried
        fine_index = (time_step_index + 1) * spacing - 1
        chosen = points[None, :] == fine_index[:, None]
        forcing = jnp.einsum(
            "qf,qfcn->qcn", chosen.astype(jnp.bfloat16), source, preferred_element_type=jnp.float32
        )
        injected = coupling[:, :, None] * jnp.einsum(
            "qf,qjfc->qjc", chosen.astype(jnp.float32), driven, precision=lax.Precision.HIGHEST
        )
        spread = spread_ports(jnp.swapaxes(injected, 1, 2), stride)
        loop_argument = (current + spacing_float[:, None, None] * (forcing + spread)).astype(
            jnp.bfloat16
        )
        loop_argument = lax.optimization_barrier(loop_argument)
        diagonal_term = inverse_diag[:, None, :] * loop_argument.astype(jnp.float32)
        updated = contract(diagonal_term, lax.all_gather(loop_argument, "blk", axis=2, tiled=True))
        active = time_step_index < step_total
        updated = jnp.where(active[:, None, None], updated, current)
        port_values = updated.reshape(sub_dev, corners, ports_block, stride)[:, :, :, 0]
        sample_times = lax.dynamic_update_index_in_dim(
            sample_times, port_values, time_step_index, 1
        )
        return (updated, sample_times)

    sample_times = jnp.zeros((sub_dev, refined_points, corners, ports_block), jnp.float32)
    last_state, sample_times = lax.fori_loop(
        0, refined_points, advance, (initial_state, sample_times)
    )
    kept_values = (points[None, :, None] // spacing[:, None, None] == points[None, None, :]).astype(
        jnp.float32
    )
    waveform = jnp.einsum(
        "qfk,qkcp->qpfc", kept_values, sample_times, precision=lax.Precision.HIGHEST
    )
    return (last_state, waveform.reshape(sub_dev, ports_block, refined_points * corners))


def shards(
    initial_state,
    source,
    inverse_diag,
    inverse_off,
    coupling,
    initial_waves,
    bucket,
    partner,
    position_of,
):
    refined_points = source.shape[1]
    subs_all = position_of.shape[0]
    identities = jnp.arange(subs_all, dtype=jnp.int32)
    located = jnp.sum(
        jnp.where(partner[:, :, None] == identities[None, None, :], position_of[None, None, :], 0),
        axis=2,
    )
    selector = (located[:, :, None] == identities[None, None, :]).astype(jnp.bfloat16)
    step_total = step_count(bucket, refined_points)
    spacing = refined_points // step_total
    waves = initial_waves
    for sweep_index in range(SWEEPS):
        incoming = port_fetch(waves, selector)
        last_state, waveform = run_together(
            initial_state,
            source,
            inverse_diag,
            inverse_off,
            coupling,
            step_total,
            spacing,
            incoming,
        )
        waves = waveform.astype(jnp.bfloat16)
    return (last_state, waveform)


def solution(mesh):
    return jax.shard_map(
        shards,
        mesh=mesh,
        in_specs=(
            P("sub", None, "blk"),
            P("sub", None, None, "blk"),
            P("sub", "blk"),
            P("sub", None, "blk"),
            P("sub", "blk"),
            P("sub", "blk", None),
            P("sub"),
            P("sub", "blk"),
            P(),
        ),
        out_specs=(P("sub", None, "blk"), P("sub", "blk", None)),
        check_vma=False,
    )
```

profile of v0, /device:TPU:0, one launch (start us, length us, event | category | flops | bytes accessed | tf_op | source)
XLA Modules:
  0.0 216.6 jit_solution(17633719554943924317)
XLA Ops:
  3.0 32.8 %all_gather.26 = bf16[8,32,512]{2,1,0:T(8,128)(2,1)S(1)} all-gather(bf16[1,32,512]{2,1,0:T(8,128)(2,1)} %param.20), channel_id=1, replica_groups=mesh['sub'=8,'blk'=4] {'sub'}, dimensions={0}, use_global_device_ids=true | all-gather | bytes 294912 | tf_op jit(solution)/shard_map/all_gather | solution.py:21
  36.2 73.8 %while.36 = (s32[]{:T(128)}, f32[1,64,512]{2,1,0:T(8,128)S(1)}, f32[1,8,64,32]{2,3,1,0:T(8,128)S(1)}, s32[1]{0:T(128)}, f32[1,512]{1,0:T(1,128)}, /*index=5*/f32...) while((s32[]{:T(128)}, f32[1,64,512]{2,1,0:T(8,128)S(1)}, ...), condition=%wide.region_2.3_spmd.clone, body=%wide.region_1.2_spmd.clone.sunk | while | flops 135202832 | bytes 13330811 | solution.py:73
  37.4 1.4 fusion.101
  38.9 5.8 %all_gather.32 = bf16[1,64,2048]{2,1,0:T(8,128)(2,1)S(1)} all-gather(bf16[1,64,512]{2,1,0:T(8,128)(2,1)S(1)} %fusion.102), channel_id=1, replica_groups=mesh['sub'=8,'blk'=4] {'blk'}, dimensions={2}, use_global_device_ids=true | all-gather | bytes 327680 | tf_op jit(solution)/shard_map/while/body/eval_jaxpr/all_gather | solution.py:63
  46.6 1.4 fusion.101
  48.1 5.9 %all_gather.32 = bf16[1,64,2048]{2,1,0:T(8,128)(2,1)S(1)} all-gather(bf16[1,64,512]{2,1,0:T(8,128)(2,1)S(1)} %fusion.102), channel_id=1, replica_groups=mesh['sub'=8,'blk'=4] {'blk'}, dimensions={2}, use_global_device_ids=true | all-gather | bytes 327680 | tf_op jit(solution)/shard_map/while/body/eval_jaxpr/all_gather | solution.py:63
  55.8 1.4 fusion.101
  57.3 5.9 %all_gather.32 = bf16[1,64,2048]{2,1,0:T(8,128)(2,1)S(1)} all-gather(bf16[1,64,512]{2,1,0:T(8,128)(2,1)S(1)} %fusion.102), channel_id=1, replica_groups=mesh['sub'=8,'blk'=4] {'blk'}, dimensions={2}, use_global_device_ids=true | all-gather | bytes 327680 | tf_op jit(solution)/shard_map/while/body/eval_jaxpr/all_gather | solution.py:63
  65.1 1.4 fusion.101
  66.6 5.9 %all_gather.32 = bf16[1,64,2048]{2,1,0:T(8,128)(2,1)S(1)} all-gather(bf16[1,64,512]{2,1,0:T(8,128)(2,1)S(1)} %fusion.102), channel_id=1, replica_groups=mesh['sub'=8,'blk'=4] {'blk'}, dimensions={2}, use_global_device_ids=true | all-gather | bytes 327680 | tf_op jit(solution)/shard_map/while/body/eval_jaxpr/all_gather | solution.py:63
  75.8 5.9 %all_gather.32 = bf16[1,64,2048]{2,1,0:T(8,128)(2,1)S(1)} all-gather(bf16[1,64,512]{2,1,0:T(8,128)(2,1)S(1)} %fusion.102), channel_id=1, replica_groups=mesh['sub'=8,'blk'=4] {'blk'}, dimensions={2}, use_global_device_ids=true | all-gather | bytes 327680 | tf_op jit(solution)/shard_map/while/body/eval_jaxpr/all_gather | solution.py:63
  85.0 5.9 %all_gather.32 = bf16[1,64,2048]{2,1,0:T(8,128)(2,1)S(1)} all-gather(bf16[1,64,512]{2,1,0:T(8,128)(2,1)S(1)} %fusion.102), channel_id=1, replica_groups=mesh['sub'=8,'blk'=4] {'blk'}, dimensions={2}, use_global_device_ids=true | all-gather | bytes 327680 | tf_op jit(solution)/shard_map/while/body/eval_jaxpr/all_gather | solution.py:63
  94.3 5.9 %all_gather.32 = bf16[1,64,2048]{2,1,0:T(8,128)(2,1)S(1)} all-gather(bf16[1,64,512]{2,1,0:T(8,128)(2,1)S(1)} %fusion.102), channel_id=1, replica_groups=mesh['sub'=8,'blk'=4] {'blk'}, dimensions={2}, use_global_device_ids=true | all-gather | bytes 327680 | tf_op jit(solution)/shard_map/while/body/eval_jaxpr/all_gather | solution.py:63
  103.5 5.9 %all_gather.32 = bf16[1,64,2048]{2,1,0:T(8,128)(2,1)S(1)} all-gather(bf16[1,64,512]{2,1,0:T(8,128)(2,1)S(1)} %fusion.102), channel_id=1, replica_groups=mesh['sub'=8,'blk'=4] {'blk'}, dimensions={2}, use_global_device_ids=true | all-gather | bytes 327680 | tf_op jit(solution)/shard_map/while/body/eval_jaxpr/all_gather | solution.py:63
  110.5 30.8 %all_gather.27 = bf16[8,32,512]{2,1,0:T(8,128)(2,1)S(1)} all-gather(bf16[1,32,512]{2,1,0:T(8,128)(2,1)S(1)} %convert_element_type.111), channel_id=1, replica_groups=mesh['sub'=8,'blk'=4] {'sub'}, dimensions={0}, use_global_device_ids=true | all-gather | bytes 294912 | tf_op jit(solution)/shard_map/all_gather | solution.py:21
  141.7 73.8 %while.37 = (s32[]{:T(128)}, f32[1,64,512]{2,1,0:T(8,128)S(1)}, f32[1,8,64,32]{2,3,1,0:T(8,128)S(1)}, s32[1]{0:T(128)}, f32[1,512]{1,0:T(1,128)}, /*index=5*/f32...) while((s32[]{:T(128)}, f32[1,64,512]{2,1,0:T(8,128)S(1)}, ...), condition=%wide.region_4.6_spmd.clone, body=%wide.region_3.5_spmd.clone.sunk | while | flops 135202832 | bytes 13330811 | solution.py:73
  144.5 5.8 %all_gather.33 = bf16[1,64,2048]{2,1,0:T(8,128)(2,1)S(1)} all-gather(bf16[1,64,512]{2,1,0:T(8,128)(2,1)S(1)} %fusion.112), channel_id=1, replica_groups=mesh['sub'=8,'blk'=4] {'blk'}, dimensions={2}, use_global_device_ids=true | all-gather | bytes 327680 | tf_op jit(solution)/shard_map/while/body/eval_jaxpr/all_gather | solution.py:63
  153.6 5.9 %all_gather.33 = bf16[1,64,2048]{2,1,0:T(8,128)(2,1)S(1)} all-gather(bf16[1,64,512]{2,1,0:T(8,128)(2,1)S(1)} %fusion.112), channel_id=1, replica_groups=mesh['sub'=8,'blk'=4] {'blk'}, dimensions={2}, use_global_device_ids=true | all-gather | bytes 327680 | tf_op jit(solution)/shard_map/while/body/eval_jaxpr/all_gather | solution.py:63
  162.9 5.9 %all_gather.33 = bf16[1,64,2048]{2,1,0:T(8,128)(2,1)S(1)} all-gather(bf16[1,64,512]{2,1,0:T(8,128)(2,1)S(1)} %fusion.112), channel_id=1, replica_groups=mesh['sub'=8,'blk'=4] {'blk'}, dimensions={2}, use_global_device_ids=true | all-gather | bytes 327680 | tf_op jit(solution)/shard_map/while/body/eval_jaxpr/all_gather | solution.py:63
  172.1 5.9 %all_gather.33 = bf16[1,64,2048]{2,1,0:T(8,128)(2,1)S(1)} all-gather(bf16[1,64,512]{2,1,0:T(8,128)(2,1)S(1)} %fusion.112), channel_id=1, replica_groups=mesh['sub'=8,'blk'=4] {'blk'}, dimensions={2}, use_global_device_ids=true | all-gather | bytes 327680 | tf_op jit(solution)/shard_map/while/body/eval_jaxpr/all_gather | solution.py:63
  181.3 5.9 %all_gather.33 = bf16[1,64,2048]{2,1,0:T(8,128)(2,1)S(1)} all-gather(bf16[1,64,512]{2,1,0:T(8,128)(2,1)S(1)} %fusion.112), channel_id=1, replica_groups=mesh['sub'=8,'blk'=4] {'blk'}, dimensions={2}, use_global_device_ids=true | all-gather | bytes 327680 | tf_op jit(solution)/shard_map/while/body/eval_jaxpr/all_gather | solution.py:63
  190.6 5.9 %all_gather.33 = bf16[1,64,2048]{2,1,0:T(8,128)(2,1)S(1)} all-gather(bf16[1,64,512]{2,1,0:T(8,128)(2,1)S(1)} %fusion.112), channel_id=1, replica_groups=mesh['sub'=8,'blk'=4] {'blk'}, dimensions={2}, use_global_device_ids=true | all-gather | bytes 327680 | tf_op jit(solution)/shard_map/while/body/eval_jaxpr/all_gather | solution.py:63
  199.8 5.9 %all_gather.33 = bf16[1,64,2048]{2,1,0:T(8,128)(2,1)S(1)} all-gather(bf16[1,64,512]{2,1,0:T(8,128)(2,1)S(1)} %fusion.112), channel_id=1, replica_groups=mesh['sub'=8,'blk'=4] {'blk'}, dimensions={2}, use_global_device_ids=true | all-gather | bytes 327680 | tf_op jit(solution)/shard_map/while/body/eval_jaxpr/all_gather | solution.py:63
  209.0 5.9 %all_gather.33 = bf16[1,64,2048]{2,1,0:T(8,128)(2,1)S(1)} all-gather(bf16[1,64,512]{2,1,0:T(8,128)(2,1)S(1)} %fusion.112), channel_id=1, replica_groups=mesh['sub'=8,'blk'=4] {'blk'}, dimensions={2}, use_global_device_ids=true | all-gather | bytes 327680 | tf_op jit(solution)/shard_map/while/body/eval_jaxpr/all_gather | solution.py:63
  (239 shorter events, 50.7 us)
Async XLA Ops:
  45.4 8.6 %copy-start = (bf16[1,2048,512]{2,1,0:T(8,128)(2,1)S(1)}, bf16[1,2048,512]{2,1,0:T(8,128)(2,1)}, u32[]{:S(2)}) copy-start(bf16[1,2048,512]{2,1,0:T(8,128)(2,1)} %get-tuple-element.845) | copy-start | bytes 6291460 | tf_op jit(solution)/shard_map/while
  45.4 8.6 %copy-start.3 = (f32[1,512]{1,0:T(1,128)S(1)}, f32[1,512]{1,0:T(1,128)}, u32[]{:S(2)}) copy-start(f32[1,512]{1,0:T(1,128)} %get-tuple-element.839) | copy-start | bytes 6148 | tf_op jit(solution)/shard_map/while
  54.6 8.6 %copy-start = (bf16[1,2048,512]{2,1,0:T(8,128)(2,1)S(1)}, bf16[1,2048,512]{2,1,0:T(8,128)(2,1)}, u32[]{:S(2)}) copy-start(bf16[1,2048,512]{2,1,0:T(8,128)(2,1)} %get-tuple-element.845) | copy-start | bytes 6291460 | tf_op jit(solution)/shard_map/while
  63.9 8.6 %copy-start = (bf16[1,2048,512]{2,1,0:T(8,128)(2,1)S(1)}, bf16[1,2048,512]{2,1,0:T(8,128)(2,1)}, u32[]{:S(2)}) copy-start(bf16[1,2048,512]{2,1,0:T(8,128)(2,1)} %get-tuple-element.845) | copy-start | bytes 6291460 | tf_op jit(solution)/shard_map/while
  63.9 8.6 %copy-start.3 = (f32[1,512]{1,0:T(1,128)S(1)}, f32[1,512]{1,0:T(1,128)}, u32[]{:S(2)}) copy-start(f32[1,512]{1,0:T(1,128)} %get-tuple-element.839) | copy-start | bytes 6148 | tf_op jit(solution)/shard_map/while
  73.1 8.6 %copy-start = (bf16[1,2048,512]{2,1,0:T(8,128)(2,1)S(1)}, bf16[1,2048,512]{2,1,0:T(8,128)(2,1)}, u32[]{:S(2)}) copy-start(bf16[1,2048,512]{2,1,0:T(8,128)(2,1)} %get-tuple-element.845) | copy-start | bytes 6291460 | tf_op jit(solution)/shard_map/while
  73.1 8.6 %copy-start.3 = (f32[1,512]{1,0:T(1,128)S(1)}, f32[1,512]{1,0:T(1,128)}, u32[]{:S(2)}) copy-start(f32[1,512]{1,0:T(1,128)} %get-tuple-element.839) | copy-start | bytes 6148 | tf_op jit(solution)/shard_map/while
  82.3 8.6 %copy-start = (bf16[1,2048,512]{2,1,0:T(8,128)(2,1)S(1)}, bf16[1,2048,512]{2,1,0:T(8,128)(2,1)}, u32[]{:S(2)}) copy-start(bf16[1,2048,512]{2,1,0:T(8,128)(2,1)} %get-tuple-element.845) | copy-start | bytes 6291460 | tf_op jit(solution)/shard_map/while
  91.6 8.6 %copy-start = (bf16[1,2048,512]{2,1,0:T(8,128)(2,1)S(1)}, bf16[1,2048,512]{2,1,0:T(8,128)(2,1)}, u32[]{:S(2)}) copy-start(bf16[1,2048,512]{2,1,0:T(8,128)(2,1)} %get-tuple-element.845) | copy-start | bytes 6291460 | tf_op jit(solution)/shard_map/while
  100.8 8.6 %copy-start = (bf16[1,2048,512]{2,1,0:T(8,128)(2,1)S(1)}, bf16[1,2048,512]{2,1,0:T(8,128)(2,1)}, u32[]{:S(2)}) copy-start(bf16[1,2048,512]{2,1,0:T(8,128)(2,1)} %get-tuple-element.845) | copy-start | bytes 6291460 | tf_op jit(solution)/shard_map/while
  150.9 8.6 %copy-start.1 = (bf16[1,2048,512]{2,1,0:T(8,128)(2,1)S(1)}, bf16[1,2048,512]{2,1,0:T(8,128)(2,1)}, u32[]{:S(2)}) copy-start(bf16[1,2048,512]{2,1,0:T(8,128)(2,1)} %get-tuple-element.887) | copy-start | bytes 6291460 | tf_op jit(solution)/shard_map/while
  150.9 8.6 %copy-start.4 = (f32[1,512]{1,0:T(1,128)S(1)}, f32[1,512]{1,0:T(1,128)}, u32[]{:S(2)}) copy-start(f32[1,512]{1,0:T(1,128)} %get-tuple-element.881) | copy-start | bytes 6148 | tf_op jit(solution)/shard_map/while
  160.1 8.6 %copy-start.1 = (bf16[1,2048,512]{2,1,0:T(8,128)(2,1)S(1)}, bf16[1,2048,512]{2,1,0:T(8,128)(2,1)}, u32[]{:S(2)}) copy-start(bf16[1,2048,512]{2,1,0:T(8,128)(2,1)} %get-tuple-element.887) | copy-start | bytes 6291460 | tf_op jit(solution)/shard_map/while
  160.2 8.6 %copy-start.4 = (f32[1,512]{1,0:T(1,128)S(1)}, f32[1,512]{1,0:T(1,128)}, u32[]{:S(2)}) copy-start(f32[1,512]{1,0:T(1,128)} %get-tuple-element.881) | copy-start | bytes 6148 | tf_op jit(solution)/shard_map/while
  169.4 8.6 %copy-start.1 = (bf16[1,2048,512]{2,1,0:T(8,128)(2,1)S(1)}, bf16[1,2048,512]{2,1,0:T(8,128)(2,1)}, u32[]{:S(2)}) copy-start(bf16[1,2048,512]{2,1,0:T(8,128)(2,1)} %get-tuple-element.887) | copy-start | bytes 6291460 | tf_op jit(solution)/shard_map/while
  169.4 8.6 %copy-start.4 = (f32[1,512]{1,0:T(1,128)S(1)}, f32[1,512]{1,0:T(1,128)}, u32[]{:S(2)}) copy-start(f32[1,512]{1,0:T(1,128)} %get-tuple-element.881) | copy-start | bytes 6148 | tf_op jit(solution)/shard_map/while
  178.6 8.6 %copy-start.1 = (bf16[1,2048,512]{2,1,0:T(8,128)(2,1)S(1)}, bf16[1,2048,512]{2,1,0:T(8,128)(2,1)}, u32[]{:S(2)}) copy-start(bf16[1,2048,512]{2,1,0:T(8,128)(2,1)} %get-tuple-element.887) | copy-start | bytes 6291460 | tf_op jit(solution)/shard_map/while
  178.6 8.6 %copy-start.4 = (f32[1,512]{1,0:T(1,128)S(1)}, f32[1,512]{1,0:T(1,128)}, u32[]{:S(2)}) copy-start(f32[1,512]{1,0:T(1,128)} %get-tuple-element.881) | copy-start | bytes 6148 | tf_op jit(solution)/shard_map/while
  187.9 8.6 %copy-start.1 = (bf16[1,2048,512]{2,1,0:T(8,128)(2,1)S(1)}, bf16[1,2048,512]{2,1,0:T(8,128)(2,1)}, u32[]{:S(2)}) copy-start(bf16[1,2048,512]{2,1,0:T(8,128)(2,1)} %get-tuple-element.887) | copy-start | bytes 6291460 | tf_op jit(solution)/shard_map/while
  187.9 8.6 %copy-start.4 = (f32[1,512]{1,0:T(1,128)S(1)}, f32[1,512]{1,0:T(1,128)}, u32[]{:S(2)}) copy-start(f32[1,512]{1,0:T(1,128)} %get-tuple-element.881) | copy-start | bytes 6148 | tf_op jit(solution)/shard_map/while
  197.1 8.6 %copy-start.1 = (bf16[1,2048,512]{2,1,0:T(8,128)(2,1)S(1)}, bf16[1,2048,512]{2,1,0:T(8,128)(2,1)}, u32[]{:S(2)}) copy-start(bf16[1,2048,512]{2,1,0:T(8,128)(2,1)} %get-tuple-element.887) | copy-start | bytes 6291460 | tf_op jit(solution)/shard_map/while
  197.1 8.6 %copy-start.4 = (f32[1,512]{1,0:T(1,128)S(1)}, f32[1,512]{1,0:T(1,128)}, u32[]{:S(2)}) copy-start(f32[1,512]{1,0:T(1,128)} %get-tuple-element.881) | copy-start | bytes 6148 | tf_op jit(solution)/shard_map/while
  206.3 8.6 %copy-start.1 = (bf16[1,2048,512]{2,1,0:T(8,128)(2,1)S(1)}, bf16[1,2048,512]{2,1,0:T(8,128)(2,1)}, u32[]{:S(2)}) copy-start(bf16[1,2048,512]{2,1,0:T(8,128)(2,1)} %get-tuple-element.887) | copy-start | bytes 6291460 | tf_op jit(solution)/shard_map/while
  206.3 8.6 %copy-start.4 = (f32[1,512]{1,0:T(1,128)S(1)}, f32[1,512]{1,0:T(1,128)}, u32[]{:S(2)}) copy-start(f32[1,512]{1,0:T(1,128)} %get-tuple-element.881) | copy-start | bytes 6148 | tf_op jit(solution)/shard_map/while
  (9 other events, 69.1 us)
where the time goes:
time: 217 us
  blocking collectives  157 us (72%)
  matrix products  35 us (16%)
  other arithmetic  15 us (7%)
  local copies, waits for them, and re-layouts  6.51 us (3%)
    all_gather x16, blocking collectives, advance(): lax.all_gather(loop_argument, 'blk', axis=2, tiled=True)  93.5 us
    all_gather x2, blocking collectives, port_fetch(): lax.all_gather(waves, 'sub', axis=0, tiled=True)  63.5 us
    dot_general x16, matrix products, advance(): jnp.einsum('qf,qfcn->qcn', chosen.astype(jnp.bfloat16), source, preferred...  23.2 us
    mul x16, other arithmetic, advance(): coupling[:, :, None]  13.5 us
    dot_general x16, matrix products, contract(): jnp.einsum('qcn,qnm->qcm', shard_rows, inverse_off, preferred_element_typ...  7.7 us

commit v1 on v0

--- a/solution.py
+++ b/solution.py
@@ -4,6 +4,18 @@
 from jax.sharding import PartitionSpec as P
 
 SWEEPS = 2
+
+
+def product_in_turn(array, axis, dim, product):
+    size, here = (lax.axis_size(axis), lax.axis_index(axis))
+    left = [(i, (i - 1) % size) for i in range(size)]
+    span = array.shape[dim]
+    carried = array
+    so_far = product(carried, here * span)
+    for lap in range(1, size):
+        carried = lax.ppermute(carried, axis, left)
+        so_far = so_far + product(carried, (here + lap) % size * span)
+    return so_far
 
 
 def step_count(bucket, refined_points):
@@ -15,11 +27,16 @@
 
 
 def port_fetch(waves, selector):
-    return jnp.einsum(
-        "qjr,rjc->qjc",
-        selector,
-        lax.all_gather(waves, "sub", axis=0, tiled=True),
-        preferred_element_type=jnp.float32,
+    return product_in_turn(
+        waves,
+        "sub",
+        0,
+        lambda own_block, offset: jnp.einsum(
+            "qjr,rjc->qjc",
+            lax.dynamic_slice_in_dim(selector, offset, own_block.shape[0], axis=2),
+            own_block,
+            preferred_element_type=jnp.float32,
+        ),
     ).astype(jnp.bfloat16)
 
 

time: 217 us -> 247 us (1.14)
  starting transfers between devices: 0 us -> 71.3 us
  blocking collectives: 157 us -> 93.5 us
  waiting for transfers between devices: 0 us -> 21 us
    ppermute x0 -> x14, starting transfers between devices: none -> 71.3 us  [product_in_turn(): carried = lax.ppermute(carried, axis, left)]
    all_gather x2 -> x0, blocking collectives: 63.5 us -> none  [port_fetch(): lax.all_gather(waves, 'sub', axis=0, tiled=True)]
    ppermute x0 -> x14, waiting for transfers between devices: none -> 21 us  [product_in_turn(): carried = lax.ppermute(carried, axis, left)]
  transfers between devices with their start and end apart: 0 -> 14, of which waited for: 0 -> 14; matrix products, arithmetic and copies ran while one was open for 0% -> 0% of each run, Pallas kernels for 0% -> 0%
where the time goes in v1:
time: 247 us; the launch traced here: 246 us
  blocking collectives  93.5 us (38%)
  starting transfers between devices  71.3 us (29%)
  matrix products  34.5 us (14%)
  waiting for transfers between devices  21 us (9%)
  other arithmetic  15.9 us (6%)
  local copies, waits for them, and re-layouts  6.61 us (3%)
    all_gather x16, blocking collectives, advance(): lax.all_gather(loop_argument, 'blk', axis=2, tiled=True)  93.5 us
    ppermute x14, starting transfers between devices, product_in_turn(): carried = lax.ppermute(carried, axis, left)  71.3 us
    dot_general x16, matrix products, advance(): jnp.einsum('qf,qfcn->qcn', chosen.astype(jnp.bfloat16), source, preferred...  23.2 us
    ppermute x14, waiting for transfers between devices, product_in_turn(): carried = lax.ppermute(carried, axis, left)  21 us
    mul x16, other arithmetic, advance(): coupling[:, :, None]  13.5 us
    dot_general x16, matrix products, contract(): jnp.einsum('qcn,qnm->qcm', shard_rows, inverse_off, preferred_element_typ...  7.7 us
  transfers between devices with their start and end apart: 14, of which 14 were waited for; matrix products, arithmetic and copies ran while one was open for 0% of the time, Pallas kernels for 0%

profile of v1, /device:TPU:0, one launch (start us, length us, event | category | flops | bytes accessed | tf_op | source)
XLA Modules:
  0.0 245.8 jit_solution(10093438271665496197)
XLA Ops:
  1.5 6.0 %collective-permute-start = (bf16[1,32,512]{2,1,0:T(8,128)(2,1)}, bf16[1,32,512]{2,1,0:T(8,128)(2,1)S(1)}, u32[]{:S(2)}, u32[]{:S(2)}) collective-permute-start(bf16[1,32,512]{2,1,0:T(8,128)(2,1)} %param.20), channel_id=1, source_target_pairs={{0,28},{4,0},{8,4},{12,8},{16,12},{20,16},{24,20},{28,24},{1,29},{... | collective-permute-start | bytes 98312 | tf_op jit(solution)/shard_map/ppermute | solution.py:16
  16.0 5.0 %collective-permute-start.2 = (bf16[1,32,512]{2,1,0:T(8,128)(2,1)S(1)}, bf16[1,32,512]{2,1,0:T(8,128)(2,1)S(1)}, u32[]{:S(2)}, u32[]{:S(2)}) collective-permute-start(bf16[1,32,512]{2,1,0:T(8,128)(2,1)S(1)} %collective-permute-done.1), channel_id=1, source_target_pairs={{0,28},{4,0},{8,4},{12,8},{16,12},{20,16},{24,20},{28,24},{1,29},{... | collective-permute-start | bytes 98312 | tf_op jit(solution)/shard_map/ppermute | solution.py:16
  22.6 5.0 %collective-permute-start.3 = (bf16[1,32,512]{2,1,0:T(8,128)(2,1)S(1)}, bf16[1,32,512]{2,1,0:T(8,128)(2,1)S(1)}, u32[]{:S(2)}, u32[]{:S(2)}) collective-permute-start(bf16[1,32,512]{2,1,0:T(8,128)(2,1)S(1)} %collective-permute-done.2), channel_id=1, source_target_pairs={{0,28},{4,0},{8,4},{12,8},{16,12},{20,16},{24,20},{28,24},{1,29},{... | collective-permute-start | bytes 98312 | tf_op jit(solution)/shard_map/ppermute | solution.py:16
  35.8 5.1 %collective-permute-start.5 = (bf16[1,32,512]{2,1,0:T(8,128)(2,1)S(1)}, bf16[1,32,512]{2,1,0:T(8,128)(2,1)S(1)}, u32[]{:S(2)}, u32[]{:S(2)}) collective-permute-start(bf16[1,32,512]{2,1,0:T(8,128)(2,1)S(1)} %collective-permute-done.4), channel_id=1, source_target_pairs={{0,28},{4,0},{8,4},{12,8},{16,12},{20,16},{24,20},{28,24},{1,29},{... | collective-permute-start | bytes 98312 | tf_op jit(solution)/shard_map/ppermute | solution.py:16
  50.1 73.8 %while.36 = (s32[]{:T(128)}, f32[1,64,512]{2,1,0:T(8,128)S(1)}, f32[1,8,64,32]{2,3,1,0:T(8,128)S(1)}, s32[1]{0:T(128)}, f32[1,512]{1,0:T(1,128)}, /*index=5*/f32...) while((s32[]{:T(128)}, f32[1,64,512]{2,1,0:T(8,128)S(1)}, ...), condition=%wide.region_2.3_spmd.clone, body=%wide.region_1.2_spmd.clone.sunk | while | flops 135202832 | bytes 13330811 | solution.py:90
  52.8 5.8 %all_gather.24 = bf16[1,64,2048]{2,1,0:T(8,128)(2,1)S(1)} all-gather(bf16[1,64,512]{2,1,0:T(8,128)(2,1)S(1)} %fusion.127), channel_id=1, replica_groups=mesh['sub'=8,'blk'=4] {'blk'}, dimensions={2}, use_global_device_ids=true | all-gather | bytes 327680 | tf_op jit(solution)/shard_map/while/body/eval_jaxpr/all_gather | solution.py:80
  62.0 5.9 %all_gather.24 = bf16[1,64,2048]{2,1,0:T(8,128)(2,1)S(1)} all-gather(bf16[1,64,512]{2,1,0:T(8,128)(2,1)S(1)} %fusion.127), channel_id=1, replica_groups=mesh['sub'=8,'blk'=4] {'blk'}, dimensions={2}, use_global_device_ids=true | all-gather | bytes 327680 | tf_op jit(solution)/shard_map/while/body/eval_jaxpr/all_gather | solution.py:80
  71.2 5.9 %all_gather.24 = bf16[1,64,2048]{2,1,0:T(8,128)(2,1)S(1)} all-gather(bf16[1,64,512]{2,1,0:T(8,128)(2,1)S(1)} %fusion.127), channel_id=1, replica_groups=mesh['sub'=8,'blk'=4] {'blk'}, dimensions={2}, use_global_device_ids=true | all-gather | bytes 327680 | tf_op jit(solution)/shard_map/while/body/eval_jaxpr/all_gather | solution.py:80
  80.5 5.9 %all_gather.24 = bf16[1,64,2048]{2,1,0:T(8,128)(2,1)S(1)} all-gather(bf16[1,64,512]{2,1,0:T(8,128)(2,1)S(1)} %fusion.127), channel_id=1, replica_groups=mesh['sub'=8,'blk'=4] {'blk'}, dimensions={2}, use_global_device_ids=true | all-gather | bytes 327680 | tf_op jit(solution)/shard_map/while/body/eval_jaxpr/all_gather | solution.py:80
  89.7 5.9 %all_gather.24 = bf16[1,64,2048]{2,1,0:T(8,128)(2,1)S(1)} all-gather(bf16[1,64,512]{2,1,0:T(8,128)(2,1)S(1)} %fusion.127), channel_id=1, replica_groups=mesh['sub'=8,'blk'=4] {'blk'}, dimensions={2}, use_global_device_ids=true | all-gather | bytes 327680 | tf_op jit(solution)/shard_map/while/body/eval_jaxpr/all_gather | solution.py:80
  98.9 5.9 %all_gather.24 = bf16[1,64,2048]{2,1,0:T(8,128)(2,1)S(1)} all-gather(bf16[1,64,512]{2,1,0:T(8,128)(2,1)S(1)} %fusion.127), channel_id=1, replica_groups=mesh['sub'=8,'blk'=4] {'blk'}, dimensions={2}, use_global_device_ids=true | all-gather | bytes 327680 | tf_op jit(solution)/shard_map/while/body/eval_jaxpr/all_gather | solution.py:80
  108.2 5.9 %all_gather.24 = bf16[1,64,2048]{2,1,0:T(8,128)(2,1)S(1)} all-gather(bf16[1,64,512]{2,1,0:T(8,128)(2,1)S(1)} %fusion.127), channel_id=1, replica_groups=mesh['sub'=8,'blk'=4] {'blk'}, dimensions={2}, use_global_device_ids=true | all-gather | bytes 327680 | tf_op jit(solution)/shard_map/while/body/eval_jaxpr/all_gather | solution.py:80
  117.4 5.9 %all_gather.24 = bf16[1,64,2048]{2,1,0:T(8,128)(2,1)S(1)} all-gather(bf16[1,64,512]{2,1,0:T(8,128)(2,1)S(1)} %fusion.127), channel_id=1, replica_groups=mesh['sub'=8,'blk'=4] {'blk'}, dimensions={2}, use_global_device_ids=true | all-gather | bytes 327680 | tf_op jit(solution)/shard_map/while/body/eval_jaxpr/all_gather | solution.py:80
  124.3 5.1 %collective-permute-start.7 = (bf16[1,32,512]{2,1,0:T(8,128)(2,1)S(1)}, bf16[1,32,512]{2,1,0:T(8,128)(2,1)S(1)}, u32[]{:S(2)}, u32[]{:S(2)}) collective-permute-start(bf16[1,32,512]{2,1,0:T(8,128)(2,1)S(1)} %convert_element_type.109), channel_id=1, source_target_pairs={{0,28},{4,0},{8,4},{12,8},{16,12},{20,16},{24,20},{28,24},{1,29},{... | collective-permute-start | bytes 98312 | tf_op jit(solution)/shard_map/ppermute | solution.py:16
  157.4 5.1 %collective-permute-start.12 = (bf16[1,32,512]{2,1,0:T(8,128)(2,1)S(1)}, bf16[1,32,512]{2,1,0:T(8,128)(2,1)S(1)}, u32[]{:S(2)}, u32[]{:S(2)}) collective-permute-start(bf16[1,32,512]{2,1,0:T(8,128)(2,1)S(1)} %collective-permute-done.11), channel_id=1, source_target_pairs={{0,28},{4,0},{8,4},{12,8},{16,12},{20,16},{24,20},{28,24},{1,29},{... | collective-permute-start | bytes 98312 | tf_op jit(solution)/shard_map/ppermute | solution.py:16
  171.0 73.8 %while.37 = (s32[]{:T(128)}, f32[1,64,512]{2,1,0:T(8,128)S(1)}, f32[1,8,64,32]{2,3,1,0:T(8,128)S(1)}, s32[1]{0:T(128)}, f32[1,512]{1,0:T(1,128)}, /*index=5*/f32...) while((s32[]{:T(128)}, f32[1,64,512]{2,1,0:T(8,128)S(1)}, ...), condition=%wide.region_4.6_spmd.clone, body=%wide.region_3.5_spmd.clone.sunk | while | flops 135202832 | bytes 13330811 | solution.py:90
  173.7 5.8 %all_gather.25 = bf16[1,64,2048]{2,1,0:T(8,128)(2,1)S(1)} all-gather(bf16[1,64,512]{2,1,0:T(8,128)(2,1)S(1)} %fusion.137), channel_id=1, replica_groups=mesh['sub'=8,'blk'=4] {'blk'}, dimensions={2}, use_global_device_ids=true | all-gather | bytes 327680 | tf_op jit(solution)/shard_map/while/body/eval_jaxpr/all_gather | solution.py:80
  182.9 5.9 %all_gather.25 = bf16[1,64,2048]{2,1,0:T(8,128)(2,1)S(1)} all-gather(bf16[1,64,512]{2,1,0:T(8,128)(2,1)S(1)} %fusion.137), channel_id=1, replica_groups=mesh['sub'=8,'blk'=4] {'blk'}, dimensions={2}, use_global_device_ids=true | all-gather | bytes 327680 | tf_op jit(solution)/shard_map/while/body/eval_jaxpr/all_gather | solution.py:80
  192.1 5.9 %all_gather.25 = bf16[1,64,2048]{2,1,0:T(8,128)(2,1)S(1)} all-gather(bf16[1,64,512]{2,1,0:T(8,128)(2,1)S(1)} %fusion.137), channel_id=1, replica_groups=mesh['sub'=8,'blk'=4] {'blk'}, dimensions={2}, use_global_device_ids=true | all-gather | bytes 327680 | tf_op jit(solution)/shard_map/while/body/eval_jaxpr/all_gather | solution.py:80
  201.3 5.9 %all_gather.25 = bf16[1,64,2048]{2,1,0:T(8,128)(2,1)S(1)} all-gather(bf16[1,64,512]{2,1,0:T(8,128)(2,1)S(1)} %fusion.137), channel_id=1, replica_groups=mesh['sub'=8,'blk'=4] {'blk'}, dimensions={2}, use_global_device_ids=true | all-gather | bytes 327680 | tf_op jit(solution)/shard_map/while/body/eval_jaxpr/all_gather | solution.py:80
  210.6 5.9 %all_gather.25 = bf16[1,64,2048]{2,1,0:T(8,128)(2,1)S(1)} all-gather(bf16[1,64,512]{2,1,0:T(8,128)(2,1)S(1)} %fusion.137), channel_id=1, replica_groups=mesh['sub'=8,'blk'=4] {'blk'}, dimensions={2}, use_global_device_ids=true | all-gather | bytes 327680 | tf_op jit(solution)/shard_map/while/body/eval_jaxpr/all_gather | solution.py:80
  219.8 5.9 %all_gather.25 = bf16[1,64,2048]{2,1,0:T(8,128)(2,1)S(1)} all-gather(bf16[1,64,512]{2,1,0:T(8,128)(2,1)S(1)} %fusion.137), channel_id=1, replica_groups=mesh['sub'=8,'blk'=4] {'blk'}, dimensions={2}, use_global_device_ids=true | all-gather | bytes 327680 | tf_op jit(solution)/shard_map/while/body/eval_jaxpr/all_gather | solution.py:80
  229.0 5.9 %all_gather.25 = bf16[1,64,2048]{2,1,0:T(8,128)(2,1)S(1)} all-gather(bf16[1,64,512]{2,1,0:T(8,128)(2,1)S(1)} %fusion.137), channel_id=1, replica_groups=mesh['sub'=8,'blk'=4] {'blk'}, dimensions={2}, use_global_device_ids=true | all-gather | bytes 327680 | tf_op jit(solution)/shard_map/while/body/eval_jaxpr/all_gather | solution.py:80
  238.3 5.9 %all_gather.25 = bf16[1,64,2048]{2,1,0:T(8,128)(2,1)S(1)} all-gather(bf16[1,64,512]{2,1,0:T(8,128)(2,1)S(1)} %fusion.137), channel_id=1, replica_groups=mesh['sub'=8,'blk'=4] {'blk'}, dimensions={2}, use_global_device_ids=true | all-gather | bytes 327680 | tf_op jit(solution)/shard_map/while/body/eval_jaxpr/all_gather | solution.py:80
  (265 shorter events, 118.0 us)
Async XLA Ops:
  1.5 7.9 %collective-permute-start = (bf16[1,32,512]{2,1,0:T(8,128)(2,1)}, bf16[1,32,512]{2,1,0:T(8,128)(2,1)S(1)}, u32[]{:S(2)}, u32[]{:S(2)}) collective-permute-start(bf16[1,32,512]{2,1,0:T(8,128)(2,1)} %param.20), channel_id=1, source_target_pairs={{0,28},{4,0},{8,4},{12,8},{16,12},{20,16},{24,20},{28,24},{1,29},{... | collective-permute-start | bytes 98312 | tf_op jit(solution)/shard_map/ppermute | solution.py:16
  9.5 6.5 %collective-permute-start.1 = (bf16[1,32,512]{2,1,0:T(8,128)(2,1)S(1)}, bf16[1,32,512]{2,1,0:T(8,128)(2,1)S(1)}, u32[]{:S(2)}, u32[]{:S(2)}) collective-permute-start(bf16[1,32,512]{2,1,0:T(8,128)(2,1)S(1)} %collective-permute-done), channel_id=1, source_target_pairs={{0,28},{4,0},{8,4},{12,8},{16,12},{20,16},{24,20},{28,24},{1,29},{... | collective-permute-start | bytes 98312 | tf_op jit(solution)/shard_map/ppermute | solution.py:16
  16.0 6.6 %collective-permute-start.2 = (bf16[1,32,512]{2,1,0:T(8,128)(2,1)S(1)}, bf16[1,32,512]{2,1,0:T(8,128)(2,1)S(1)}, u32[]{:S(2)}, u32[]{:S(2)}) collective-permute-start(bf16[1,32,512]{2,1,0:T(8,128)(2,1)S(1)} %collective-permute-done.1), channel_id=1, source_target_pairs={{0,28},{4,0},{8,4},{12,8},{16,12},{20,16},{24,20},{28,24},{1,29},{... | collective-permute-start | bytes 98312 | tf_op jit(solution)/shard_map/ppermute | solution.py:16
  22.6 6.6 %collective-permute-start.3 = (bf16[1,32,512]{2,1,0:T(8,128)(2,1)S(1)}, bf16[1,32,512]{2,1,0:T(8,128)(2,1)S(1)}, u32[]{:S(2)}, u32[]{:S(2)}) collective-permute-start(bf16[1,32,512]{2,1,0:T(8,128)(2,1)S(1)} %collective-permute-done.2), channel_id=1, source_target_pairs={{0,28},{4,0},{8,4},{12,8},{16,12},{20,16},{24,20},{28,24},{1,29},{... | collective-permute-start | bytes 98312 | tf_op jit(solution)/shard_map/ppermute | solution.py:16
  29.2 6.6 %collective-permute-start.4 = (bf16[1,32,512]{2,1,0:T(8,128)(2,1)S(1)}, bf16[1,32,512]{2,1,0:T(8,128)(2,1)S(1)}, u32[]{:S(2)}, u32[]{:S(2)}) collective-permute-start(bf16[1,32,512]{2,1,0:T(8,128)(2,1)S(1)} %collective-permute-done.3), channel_id=1, source_target_pairs={{0,28},{4,0},{8,4},{12,8},{16,12},{20,16},{24,20},{28,24},{1,29},{... | collective-permute-start | bytes 98312 | tf_op jit(solution)/shard_map/ppermute | solution.py:16
  35.8 6.7 %collective-permute-start.5 = (bf16[1,32,512]{2,1,0:T(8,128)(2,1)S(1)}, bf16[1,32,512]{2,1,0:T(8,128)(2,1)S(1)}, u32[]{:S(2)}, u32[]{:S(2)}) collective-permute-start(bf16[1,32,512]{2,1,0:T(8,128)(2,1)S(1)} %collective-permute-done.4), channel_id=1, source_target_pairs={{0,28},{4,0},{8,4},{12,8},{16,12},{20,16},{24,20},{28,24},{1,29},{... | collective-permute-start | bytes 98312 | tf_op jit(solution)/shard_map/ppermute | solution.py:16
  42.5 6.6 %collective-permute-start.6 = (bf16[1,32,512]{2,1,0:T(8,128)(2,1)S(1)}, bf16[1,32,512]{2,1,0:T(8,128)(2,1)S(1)}, u32[]{:S(2)}, u32[]{:S(2)}) collective-permute-start(bf16[1,32,512]{2,1,0:T(8,128)(2,1)S(1)} %collective-permute-done.5), channel_id=1, source_target_pairs={{0,28},{4,0},{8,4},{12,8},{16,12},{20,16},{24,20},{28,24},{1,29},{... | collective-permute-start | bytes 98312 | tf_op jit(solution)/shard_map/ppermute | solution.py:16
  59.3 8.6 %copy-start = (bf16[1,2048,512]{2,1,0:T(8,128)(2,1)S(1)}, bf16[1,2048,512]{2,1,0:T(8,128)(2,1)}, u32[]{:S(2)}) copy-start(bf16[1,2048,512]{2,1,0:T(8,128)(2,1)} %get-tuple-element.853) | copy-start | bytes 6291460 | tf_op jit(solution)/shard_map/while
  68.5 8.6 %copy-start = (bf16[1,2048,512]{2,1,0:T(8,128)(2,1)S(1)}, bf16[1,2048,512]{2,1,0:T(8,128)(2,1)}, u32[]{:S(2)}) copy-start(bf16[1,2048,512]{2,1,0:T(8,128)(2,1)} %get-tuple-element.853) | copy-start | bytes 6291460 | tf_op jit(solution)/shard_map/while
  77.8 8.6 %copy-start = (bf16[1,2048,512]{2,1,0:T(8,128)(2,1)S(1)}, bf16[1,2048,512]{2,1,0:T(8,128)(2,1)}, u32[]{:S(2)}) copy-start(bf16[1,2048,512]{2,1,0:T(8,128)(2,1)} %get-tuple-element.853) | copy-start | bytes 6291460 | tf_op jit(solution)/shard_map/while
  87.0 8.6 %copy-start = (bf16[1,2048,512]{2,1,0:T(8,128)(2,1)S(1)}, bf16[1,2048,512]{2,1,0:T(8,128)(2,1)}, u32[]{:S(2)}) copy-start(bf16[1,2048,512]{2,1,0:T(8,128)(2,1)} %get-tuple-element.853) | copy-start | bytes 6291460 | tf_op jit(solution)/shard_map/while
  96.2 8.6 %copy-start = (bf16[1,2048,512]{2,1,0:T(8,128)(2,1)S(1)}, bf16[1,2048,512]{2,1,0:T(8,128)(2,1)}, u32[]{:S(2)}) copy-start(bf16[1,2048,512]{2,1,0:T(8,128)(2,1)} %get-tuple-element.853) | copy-start | bytes 6291460 | tf_op jit(solution)/shard_map/while
  105.5 8.6 %copy-start = (bf16[1,2048,512]{2,1,0:T(8,128)(2,1)S(1)}, bf16[1,2048,512]{2,1,0:T(8,128)(2,1)}, u32[]{:S(2)}) copy-start(bf16[1,2048,512]{2,1,0:T(8,128)(2,1)} %get-tuple-element.853) | copy-start | bytes 6291460 | tf_op jit(solution)/shard_map/while
  114.7 8.6 %copy-start = (bf16[1,2048,512]{2,1,0:T(8,128)(2,1)S(1)}, bf16[1,2048,512]{2,1,0:T(8,128)(2,1)}, u32[]{:S(2)}) copy-start(bf16[1,2048,512]{2,1,0:T(8,128)(2,1)} %get-tuple-element.853) | copy-start | bytes 6291460 | tf_op jit(solution)/shard_map/while
  124.3 6.7 %collective-permute-start.7 = (bf16[1,32,512]{2,1,0:T(8,128)(2,1)S(1)}, bf16[1,32,512]{2,1,0:T(8,128)(2,1)S(1)}, u32[]{:S(2)}, u32[]{:S(2)}) collective-permute-start(bf16[1,32,512]{2,1,0:T(8,128)(2,1)S(1)} %convert_element_type.109), channel_id=1, source_target_pairs={{0,28},{4,0},{8,4},{12,8},{16,12},{20,16},{24,20},{28,24},{1,29},{... | collective-permute-start | bytes 98312 | tf_op jit(solution)/shard_map/ppermute | solution.py:16
  131.0 6.6 %collective-permute-start.8 = (bf16[1,32,512]{2,1,0:T(8,128)(2,1)S(1)}, bf16[1,32,512]{2,1,0:T(8,128)(2,1)S(1)}, u32[]{:S(2)}, u32[]{:S(2)}) collective-permute-start(bf16[1,32,512]{2,1,0:T(8,128)(2,1)S(1)} %collective-permute-done.7), channel_id=1, source_target_pairs={{0,28},{4,0},{8,4},{12,8},{16,12},{20,16},{24,20},{28,24},{1,29},{... | collective-permute-start | bytes 98312 | tf_op jit(solution)/shard_map/ppermute | solution.py:16
  137.6 6.6 %collective-permute-start.9 = (bf16[1,32,512]{2,1,0:T(8,128)(2,1)S(1)}, bf16[1,32,512]{2,1,0:T(8,128)(2,1)S(1)}, u32[]{:S(2)}, u32[]{:S(2)}) collective-permute-start(bf16[1,32,512]{2,1,0:T(8,128)(2,1)S(1)} %collective-permute-done.8), channel_id=1, source_target_pairs={{0,28},{4,0},{8,4},{12,8},{16,12},{20,16},{24,20},{28,24},{1,29},{... | collective-permute-start | bytes 98312 | tf_op jit(solution)/shard_map/ppermute | solution.py:16
  144.2 6.6 %collective-permute-start.10 = (bf16[1,32,512]{2,1,0:T(8,128)(2,1)S(1)}, bf16[1,32,512]{2,1,0:T(8,128)(2,1)S(1)}, u32[]{:S(2)}, u32[]{:S(2)}) collective-permute-start(bf16[1,32,512]{2,1,0:T(8,128)(2,1)S(1)} %collective-permute-done.9), channel_id=1, source_target_pairs={{0,28},{4,0},{8,4},{12,8},{16,12},{20,16},{24,20},{28,24},{1,29},{... | collective-permute-start | bytes 98312 | tf_op jit(solution)/shard_map/ppermute | solution.py:16
  150.8 6.6 %collective-permute-start.11 = (bf16[1,32,512]{2,1,0:T(8,128)(2,1)S(1)}, bf16[1,32,512]{2,1,0:T(8,128)(2,1)S(1)}, u32[]{:S(2)}, u32[]{:S(2)}) collective-permute-start(bf16[1,32,512]{2,1,0:T(8,128)(2,1)S(1)} %collective-permute-done.10), channel_id=1, source_target_pairs={{0,28},{4,0},{8,4},{12,8},{16,12},{20,16},{24,20},{28,24},{1,29},{... | collective-permute-start | bytes 98312 | tf_op jit(solution)/shard_map/ppermute | solution.py:16
  157.4 6.7 %collective-permute-start.12 = (bf16[1,32,512]{2,1,0:T(8,128)(2,1)S(1)}, bf16[1,32,512]{2,1,0:T(8,128)(2,1)S(1)}, u32[]{:S(2)}, u32[]{:S(2)}) collective-permute-start(bf16[1,32,512]{2,1,0:T(8,128)(2,1)S(1)} %collective-permute-done.11), channel_id=1, source_target_pairs={{0,28},{4,0},{8,4},{12,8},{16,12},{20,16},{24,20},{28,24},{1,29},{... | collective-permute-start | bytes 98312 | tf_op jit(solution)/shard_map/ppermute | solution.py:16
  164.2 6.6 %collective-permute-start.13 = (bf16[1,32,512]{2,1,0:T(8,128)(2,1)S(1)}, bf16[1,32,512]{2,1,0:T(8,128)(2,1)S(1)}, u32[]{:S(2)}, u32[]{:S(2)}) collective-permute-start(bf16[1,32,512]{2,1,0:T(8,128)(2,1)S(1)} %collective-permute-done.12), channel_id=1, source_target_pairs={{0,28},{4,0},{8,4},{12,8},{16,12},{20,16},{24,20},{28,24},{1,29},{... | collective-permute-start | bytes 98312 | tf_op jit(solution)/shard_map/ppermute | solution.py:16
  189.4 8.6 %copy-start.1 = (bf16[1,2048,512]{2,1,0:T(8,128)(2,1)S(1)}, bf16[1,2048,512]{2,1,0:T(8,128)(2,1)}, u32[]{:S(2)}) copy-start(bf16[1,2048,512]{2,1,0:T(8,128)(2,1)} %get-tuple-element.895) | copy-start | bytes 6291460 | tf_op jit(solution)/shard_map/while
  207.9 8.6 %copy-start.1 = (bf16[1,2048,512]{2,1,0:T(8,128)(2,1)S(1)}, bf16[1,2048,512]{2,1,0:T(8,128)(2,1)}, u32[]{:S(2)}) copy-start(bf16[1,2048,512]{2,1,0:T(8,128)(2,1)} %get-tuple-element.895) | copy-start | bytes 6291460 | tf_op jit(solution)/shard_map/while
  235.6 8.6 %copy-start.1 = (bf16[1,2048,512]{2,1,0:T(8,128)(2,1)S(1)}, bf16[1,2048,512]{2,1,0:T(8,128)(2,1)}, u32[]{:S(2)}) copy-start(bf16[1,2048,512]{2,1,0:T(8,128)(2,1)} %get-tuple-element.895) | copy-start | bytes 6291460 | tf_op jit(solution)/shard_map/while
  (23 other events, 188.9 us)
